TPU v7x, 32 devices: a whole 2x2x4 slice. The times are simulated.
32 devices in a mesh: gx: 16 (over z, y, x), gy: 2 (over core).
Axes of the slice: x: 2, y: 2, z: 4, core: 2. Of those that a mesh axis runs over, the one named last changes fastest.
Arguments:
- node_latents: bfloat16 [16, 2, 256, 512], P('gx', 'gy'), may hold values from -6 to 6
- edge_latents: bfloat16 [16, 2, 768, 512], P('gx', 'gy'), may hold values from -6 to 6
- edge_w1: bfloat16 [1536, 512], replicated, may hold values from -0.15625 to 0.15625
- edge_b1: float32 [512], replicated, may hold values from -3 to 3
- edge_w2: bfloat16 [512, 512], replicated, may hold values from -0.25 to 0.25
- node_w1: bfloat16 [1024, 512], replicated, may hold values from -0.1875 to 0.1875
- node_b1: float32 [512], replicated, may hold values from -3 to 3
- node_w2: bfloat16 [512, 512], replicated, may hold values from -0.25 to 0.25
- node_cot: bfloat16 [16, 2, 256, 512], P('gx', 'gy'), may hold values from -6 to 6
- edge_cot: bfloat16 [16, 2, 768, 512], P('gx', 'gy'), may hold values from -6 to 6
- send_count: int32 [16, 2, 4], P('gx', 'gy'), may hold values from 0 to 2, as said below
- send_list: int32 [16, 2, 4, 2], P('gx', 'gy'), may hold values from 0 to 1
- tile_recv: int32 [16, 2, 6], P('gx', 'gy'), may hold values from 0 to 1
- tile_send: int32 [16, 2, 6], P('gx', 'gy'), may hold values from 0 to 9, as said below
- tile_perm: int32 [16, 2, 6, 128], P('gx', 'gy'), may hold values from 0 to 127, each once within a row
Outputs:
- node_out: bfloat16 [16, 2, 256, 512], P('gx', 'gy')
- node_grad: bfloat16 [16, 2, 256, 512], P('gx', 'gy')
- edge_grad: bfloat16 [16, 2, 768, 512], P('gx', 'gy')
- weight_dir: bfloat16 [1835008], P(('gx', 'gy'))
Inputs may be any that keep to these rules, and one draw needn't show every extreme that they name: `send_count`: entries for a neighbour outside the grid of partitions are 0, all others at least 1; the partition at (0, 0) sends 2 blocks to its neighbour at gx+1. `tile_send`: A value of 2 or more is a halo slot 2 + d * 2 + s that direction d's neighbour fills (s below its send count).
All inputs are finite; a program needn't handle non-finite values.
Results may differ from a plain program's by a relative error of at most 0.0075.
Values may be sent and summed in bfloat16 or wider, within the bound.
No kernel may reach another device: no remote copies, remote signals or barrier semaphores. Data moves between devices by JAX's collectives and lax.ppermute only.
A program may use at most 128 MiB of HBM per device.

v0:
```python
import jax
import jax.numpy as jnp
from jax import lax
from jax.sharding import PartitionSpec as P


def padded(block, sides, width):
    for axis, dim in sides:
        count = lax.axis_size(axis)
        forward = [(i, i + 1) for i in range(count - 1)]
        backward = [(target, source) for source, target in forward]
        low = lax.ppermute(
            lax.slice_in_dim(block, block.shape[dim] - width, None, axis=dim), axis, forward
        )
        high = lax.ppermute(lax.slice_in_dim(block, 0, width, axis=dim), axis, backward)
        block = jnp.concatenate([low, block, high], axis=dim)
    return block


def silu_slope(values):
    logistic = jax.nn.sigmoid(values)
    return logistic * (1.0 + values * (1.0 - logistic))


def layer_norm(values):
    center = values - jnp.mean(values, axis=-1, keepdims=True)
    inverse_rms = lax.rsqrt(jnp.mean(center * center, axis=-1, keepdims=True) + 1e-05)
    return (center * inverse_rms, inverse_rms)


def norm_back(normed, inverse_rms, upstream):
    return inverse_rms * (
        upstream
        - jnp.mean(upstream, axis=-1, keepdims=True)
        - normed * jnp.mean(upstream * normed, axis=-1, keepdims=True)
    )


def inner_rows(factor, second):
    return lax.dot_general(
        factor, second, (((0,), (0,)), ((), ())), preferred_element_type=jnp.float32
    )


def times_transposed(factor, second):
    return lax.dot_general(
        factor, second, (((1,), (1,)), ((), ())), preferred_element_type=jnp.float32
    )


def matmul(factor, second):
    return jnp.dot(factor, second, preferred_element_type=jnp.float32)


def fetch_halo(packed):
    row_halo = padded(jnp.stack([packed[1], packed[0]]), (("gx", 0),), 1)
    col_halo = padded(jnp.stack([packed[3], packed[2]]), (("gy", 0),), 1)
    return jnp.concatenate([row_halo[0], row_halo[3], col_halo[0], col_halo[3]], axis=0)


def return_partials(halo_part):
    row_back = padded(
        jnp.stack([halo_part[0], halo_part[1]]).astype(jnp.bfloat16), (("gx", 0),), 1
    ).astype(jnp.float32)
    col_back = padded(
        jnp.stack([halo_part[2], halo_part[3]]).astype(jnp.bfloat16), (("gy", 0),), 1
    ).astype(jnp.float32)
    return jnp.stack([row_back[3], row_back[0], col_back[3], col_back[0]])


def on_device(
    node_latents,
    edge_latents,
    edge_w1,
    edge_b1,
    edge_w2,
    node_w1,
    node_b1,
    node_w2,
    node_cot,
    edge_cot,
    send_count,
    send_list,
    tile_recv,
    tile_send,
    tile_perm,
):
    feature = node_latents.shape[3]
    block_size = tile_perm.shape[3]
    tile_count = tile_perm.shape[2]
    slot_count = send_list.shape[3]
    node_count = node_latents.shape[2]
    block_count = node_count // block_size
    node_blocks = node_latents.reshape(block_count, block_size, feature)
    local_rows = node_latents.reshape(node_count, feature)
    edge_rows = edge_latents.reshape(tile_count * block_size, feature)
    cot_node = node_cot.reshape(node_count, feature)
    cot_edge = edge_cot.reshape(tile_count * block_size, feature)
    send_counts = send_count.reshape(4)
    send_lists = send_list.reshape(4, slot_count)
    recv_idx = tile_recv.reshape(tile_count)
    send_idx = tile_send.reshape(tile_count)
    perm_idx = tile_perm.reshape(tile_count, block_size)
    live_slots = jnp.arange(slot_count, dtype=jnp.int32)[None, :] < send_counts[:, None]
    packed = jnp.where(
        live_slots[:, :, None, None], node_blocks[send_lists], jnp.zeros((), jnp.bfloat16)
    )
    offsets = jnp.arange(block_size, dtype=jnp.int32)
    recv_rows = (recv_idx[:, None] * block_size + offsets[None, :]).reshape(-1)
    send_rows = (send_idx[:, None] * block_size + perm_idx).reshape(-1)
    h_recv = local_rows[recv_rows]
    halo_blocks = fetch_halo(packed)
    flat_ext = jnp.concatenate([node_blocks, halo_blocks], axis=0).reshape(-1, feature)
    h_send = flat_ext[send_rows]
    joined = jnp.concatenate([edge_rows, h_recv, h_send], axis=1)
    edge_affine = matmul(joined, edge_w1) + edge_b1
    edge_hidden = jax.nn.silu(edge_affine).astype(jnp.bfloat16)
    edge_linear = matmul(edge_hidden, edge_w2)
    message, edge_inv = layer_norm(edge_linear)
    recv_hot = (recv_idx[None, :] == jnp.arange(block_count, dtype=jnp.int32)[:, None]).astype(
        jnp.float32
    )
    aggregate = jnp.einsum(
        "bt,tnf->bnf",
        recv_hot,
        message.reshape(tile_count, block_size, feature),
        precision=lax.Precision.HIGHEST,
    )
    aggregate = aggregate.reshape(node_count, feature).astype(jnp.bfloat16)
    node_input = jnp.concatenate([local_rows, aggregate], axis=1)
    node_affine = matmul(node_input, node_w1) + node_b1
    node_hidden = jax.nn.silu(node_affine).astype(jnp.bfloat16)
    node_linear = matmul(node_hidden, node_w2)
    node_normed, node_inv = layer_norm(node_linear)
    node_out = (local_rows.astype(jnp.float32) + node_normed).astype(jnp.bfloat16)
    grad_node_linear = norm_back(node_normed, node_inv, cot_node.astype(jnp.float32)).astype(
        jnp.bfloat16
    )
    g_nw2 = inner_rows(node_hidden, grad_node_linear)
    grad_node_affine = (
        times_transposed(grad_node_linear, node_w2) * silu_slope(node_affine)
    ).astype(jnp.bfloat16)
    g_nw1 = inner_rows(node_input, grad_node_affine)
    grad_node_input = times_transposed(grad_node_affine, node_w1)
    grad_direct = grad_node_input[:, :feature]
    grad_aggregate = grad_node_input[:, feature:]
    grad_message = grad_aggregate[recv_rows] + cot_edge.astype(jnp.float32)
    grad_edge_linear = norm_back(message, edge_inv, grad_message).astype(jnp.bfloat16)
    g_ew2 = inner_rows(edge_hidden, grad_edge_linear)
    grad_edge_affine = (
        times_transposed(grad_edge_linear, edge_w2) * silu_slope(edge_affine)
    ).astype(jnp.bfloat16)
    g_ew1 = inner_rows(joined, grad_edge_affine)
    grad_joined = times_transposed(grad_edge_affine, edge_w1)
    grad_e = grad_joined[:, :feature]
    grad_r = grad_joined[:, feature : 2 * feature]
    grad_s = grad_joined[:, 2 * feature :]
    edge_grad = (cot_edge.astype(jnp.float32) + grad_e).astype(jnp.bfloat16)
    grad_recv = jnp.einsum(
        "bt,tnf->bnf",
        recv_hot,
        grad_r.reshape(tile_count, block_size, feature),
        precision=lax.Precision.HIGHEST,
    )
    inverse = jnp.argsort(perm_idx, axis=1)
    grad_send = jnp.take_along_axis(
        grad_s.reshape(tile_count, block_size, feature), inverse[:, :, None], axis=1
    )
    extended_count = block_count + 4 * slot_count
    send_hot = (send_idx[None, :] == jnp.arange(extended_count, dtype=jnp.int32)[:, None]).astype(
        jnp.float32
    )
    partial_sum = jnp.einsum("bt,tnf->bnf", send_hot, grad_send, precision=lax.Precision.HIGHEST)
    owned_part = (
        partial_sum[:block_count]
        + grad_recv
        + grad_direct.reshape(block_count, block_size, feature)
    )
    halo_part = partial_sum[block_count:].reshape(4, slot_count, block_size, feature)
    returned = return_partials(halo_part)
    back_hot = (
        (send_lists[:, :, None] == jnp.arange(block_count, dtype=jnp.int32)[None, None, :])
        & live_slots[:, :, None]
    ).astype(jnp.float32)
    contrib = jnp.einsum("qsb,qsnf->bnf", back_hot, returned, precision=lax.Precision.HIGHEST)
    node_grad = (
        cot_node.reshape(block_count, block_size, feature).astype(jnp.float32)
        + owned_part
        + contrib
    )
    node_grad = node_grad.astype(jnp.bfloat16).reshape(1, 1, node_count, feature)
    weight_grad = jnp.concatenate([g_ew1, g_ew2, g_nw1, g_nw2], axis=0)
    total_entries = 7 * feature * feature
    share_len = total_entries // lax.axis_size(("gx", "gy"))
    summed = lax.psum(weight_grad, ("gx", "gy"))
    bounds = [0, 3 * feature, 4 * feature, 6 * feature, 7 * feature]
    pieces = []
    for index in range(4):
        matrix = summed[bounds[index] : bounds[index + 1]]
        pieces.append(matrix * lax.rsqrt(jnp.mean(matrix * matrix) + 1e-06))
    normalized = jnp.concatenate(pieces, axis=0).reshape(total_entries)
    own_start = lax.axis_index(("gx", "gy")) * share_len
    weight_dir = lax.dynamic_slice_in_dim(normalized, own_start, share_len).astype(jnp.bfloat16)
    return (
        node_out.reshape(1, 1, node_count, feature),
        node_grad,
        edge_grad.reshape(1, 1, tile_count * block_size, feature),
        weight_dir,
    )


def solution(mesh):
    placed = (
        P("gx", "gy", None, None),
        P("gx", "gy", None, None),
        P(),
        P(),
        P(),
        P(),
        P(),
        P(),
        P("gx", "gy", None, None),
        P("gx", "gy", None, None),
        P("gx", "gy", None),
        P("gx", "gy", None, None),
        P("gx", "gy", None),
        P("gx", "gy", None),
        P("gx", "gy", None, None),
    )
    return jax.shard_map(
        on_device,
        mesh=mesh,
        in_specs=placed,
        out_specs=(
            P("gx", "gy", None, None),
            P("gx", "gy", None, None),
            P("gx", "gy", None, None),
            P(("gx", "gy")),
        ),
        check_vma=False,
    )
```

profile of v0, /device:TPU:0, one launch (start us, length us, event | category | flops | bytes accessed | tf_op | source)
XLA Modules:
  0.0 270.5 jit_solution(10264045444098275007)
XLA Ops:
  8.1 0.8 compare_select_fusion.3
  9.0 0.7 iota_compare_fusion.1
  9.8 1.6 gather_fusion.1
  11.6 1.0 fusion.59
  12.6 5.6 %collective-permute-start = (bf16[1,2,128,512]{3,2,1,0:T(8,128)(2,1)}, bf16[1,2,128,512]{3,2,1,0:T(8,128)(2,1)}, u32[]{:S(2)}, u32[]{:S(2)}) collective-permute-start(bf16[1,2,128,512]{3,2,1,0:T(8,128)(2,1)} %get-tuple-element.28), channel_id=1, source_target_pairs={{0,2},{2,4},{4,6},{6,8},{8,10},{10,12},{12,14},{14,16},{16,18},{18... | collective-permute-start | bytes 786440 | tf_op jit(solution)/shard_map/ppermute | solution.py:12
  18.1 1.3 collective-permute-start.1
  19.4 2.2 collective-permute-start.2
  21.6 1.3 collective-permute-start.3
  22.9 0.6 copy.83
  23.5 0.6 iota.34
  24.5 3.4 %gather_fusion = bf16[768,512]{1,0:T(8,128)(2,1)} fusion(bf16[256,512]{1,0:T(8,128)(2,1)S(1)} %bitcast.130, s32[1024]{0:T(1024)S(1)} %get-tuple-element.40), kind=kCustom, calls=%fused_computation | custom fusion | bytes 1575936 | tf_op jit(solution)/shard_map/gather | solution.py:111
  27.9 1.0 collective-permute-done
  28.9 1.0 bitcast_dynamic-update-slice_fusion.3
  29.9 0.9 collective-permute-done.1
  30.9 1.0 bitcast_dynamic-update-slice_fusion.2
  31.8 1.0 bitcast_dynamic-update-slice_fusion.1
  32.8 1.0 bitcast_dynamic-update-slice_fusion
  33.8 3.3 %gather_fusion.2 = bf16[768,512]{1,0:T(8,128)(2,1)} fusion(bf16[1280,512]{1,0:T(8,128)(2,1)S(1)} %bitcast.134, s32[1024]{0:T(1024)S(1)} %get-tuple-element.39), kind=kCustom, calls=%fused_computation.2 | custom fusion | bytes 1575936 | tf_op jit(solution)/shard_map/gather | solution.py:114
  37.1 4.3 %multiply_convert_fusion.2 = (bf16[768,512]{1,0:T(8,128)(2,1)S(1)}, f32[768,512]{1,0:T(8,128)}) fusion(f32[512]{0:T(512)S(1)} %copy-done.26, bf16[1536,512]{1,0:T(8,128)(2,1)S(1)} %copy-done, bf16[768,512]{1,0:T(8,128)(2,1)} %gather_fusion.2, bf16[768,512]{1,0:T(8,128)(2,1)} %gather_fusion, bf16[768,512]{1,0:T(8,128)(2,1)} %bitcast.150), kind=kOutput, calls=%fused_computation.28 | convolution fusion | flops 1217396736 | bytes 6293504 | tf_op jit(solution)/shard_map/dot_general | solution.py:52
  41.5 0.6 fusion.60
  43.3 1.9 fusion.12
  45.7 0.5 copy-done.24
  46.9 0.9 fusion.28
  47.8 1.5 fusion.54
  50.3 1.8 fusion.29
  52.1 0.9 fusion.58
  53.0 3.2 %gather_fusion.3 = f32[768,512]{1,0:T(8,128)} fusion(f32[256,512]{1,0:T(8,128)S(1)} %get-tuple-element.23, s32[1024]{0:T(1024)S(1)} %get-tuple-element.40), kind=kCustom, calls=%fused_computation.3 | custom fusion | bytes 3148800 | tf_op jit(solution)/shard_map/gather | solution.py:147
  56.1 2.7 fusion.20
  58.9 0.5 multiply_convert_fusion.1
  59.5 0.6 copy-done.10
  60.1 0.6 fusion.65
  61.1 0.5 copy-done.27
  61.7 0.9 multiply_convert_fusion
  63.3 1.4 fusion.17
  65.1 3.4 %pad_maximum_fusion = f32[3584,512]{1,0:T(8,128)} fusion(f32[512,512]{1,0:T(8,128)S(1)} %copy-done.13, f32[1024,512]{1,0:T(8,128)S(1)} %copy-done.6, f32[512,512]{1,0:T(8,128)S(1)} %fusion.65, f32[1536,512]{1,0:T(8,128)S(1)} %fusion.17), kind=kLoop, calls=%fused_computation.5 | loop fusion | flops 5505024 | bytes 14680064 | tf_op jit(solution)/shard_map/concatenate | solution.py:192
  68.6 0.7 compare_and_fusion
  69.4 0.7 fusion.33
  70.1 1.4 fusion.64
  71.5 1.9 fusion.19
  73.4 7.8 %gather_fusion.4 = f32[768,512]{1,0:T(8,128)} fusion(f32[6,128,512]{2,1,0:T(8,128)S(1)} %bitcast.133, s32[768]{0:T(1024)S(1)} %fusion.33), kind=kCustom, calls=%fused_computation.4 | custom fusion | bytes 3151872 | tf_op jit(solution)/shard_map/jit(take_along_axis)/gather | solution.py:166
  81.2 4.7 %fusion.62 = (bf16[10,128,512]{2,0,1:T(8,128)(2,1)S(1)}, f32[10,128,512]{2,0,1:T(8,128)S(1)}) fusion(f32[6,128,512]{2,1,0:T(8,128)} %bitcast.137, pred[6,128]{0,1:T(8,128)(4,1)S(1)} %copy.42, s32[6]{0:T(128)S(1)} %bitcast.149), kind=kOutput, calls=%fused_computation.139 | convolution fusion | flops 48234556 | bytes 5505816 | tf_op jit(solution)/shard_map/bt,tnf->bnf/dot_general | solution.py:173
  86.0 0.8 slice_bitcast_fusion.3
  86.8 3.4 %collective-permute-start.4 = (bf16[1,2,128,512]{3,1,2,0:T(2,128)(2,1)S(1)}, bf16[1,2,128,512]{3,1,2,0:T(2,128)(2,1)S(1)}, u32[]{:S(2)}, u32[]{:S(2)}) collective-permute-start(bf16[1,2,128,512]{3,1,2,0:T(2,128)(2,1)S(1)} %get-tuple-element.15), channel_id=1, source_target_pairs={{0,2},{2,4},{4,6},{6,8},{8,10},{10,12},{12,14},{14,16},{16,18},{18... | collective-permute-start | bytes 786440 | tf_op jit(solution)/shard_map/ppermute | solution.py:12
  90.3 1.3 collective-permute-start.5
  91.6 2.5 collective-permute-start.6
  94.1 1.5 collective-permute-start.7
  95.6 1.9 fusion.2
  97.7 6.4 %collective-permute-done.4 = bf16[1,2,128,512]{3,1,2,0:T(2,128)(2,1)S(1)} collective-permute-done((bf16[1,2,128,512]{3,1,2,0:T(2,128)(2,1)S(1)}, bf16[1,2,128,512]{3,1,2,0:T(2,128)(2,1)S(1)}, u32[]{:S(2)}, u32[]{:S(2)}) %collective-permute-start.4) | collective-permute-done | bytes 262176 | tf_op jit(solution)/shard_map/ppermute | solution.py:12
  104.1 3.6 %collective-permute-done.5 = bf16[1,2,128,512]{3,1,2,0:T(2,128)(2,1)S(1)} collective-permute-done((bf16[1,2,128,512]{3,1,2,0:T(2,128)(2,1)S(1)}, bf16[1,2,128,512]{3,1,2,0:T(2,128)(2,1)S(1)}, u32[]{:S(2)}, u32[]{:S(2)}) %collective-permute-start.5) | collective-permute-done | bytes 262176 | tf_op jit(solution)/shard_map/ppermute | solution.py:15
  107.7 0.6 maximum_convert_fusion.1
  108.4 0.6 maximum_convert_fusion
  109.0 1.1 pad_maximum_fusion.2
  110.2 3.2 %fusion.8 = f32[2,128,512]{2,0,1:T(2,128)S(1)} fusion(f32[4,2,128,512]{3,1,2,0:T(2,128)S(1)} %pad_maximum_fusion.2, pred[4,2]{0,1:T(4,128)(4,1)S(1)} %iota_compare_fusion.1, s32[4,2]{0,1:T(2,128)S(1)} %bitcast.146), kind=kOutput, calls=%fused_computation.32 | convolution fusion | flops 12582944 | bytes 2621480 | tf_op jit(solution)/shard_map/qsb,qsnf->bnf/dot_general | solution.py:185
  113.4 1.0 fusion.24
  114.4 128.1 %all-reduce.2.cloned.1.call-done = f32[3584,512]{1,0:T(8,128)} async-done(((f32[3584,512]{1,0:T(8,128)}), f32[3584,512]{1,0:T(8,128)}) %all-reduce.2.cloned.1.call-update) | async-done | bytes 7340048 | tf_op jit(solution)/shard_map/psum | solution.py:195
  242.5 3.3 %multiply_reduce_fusion = f32[]{:T(128)} fusion(f32[3584,512]{1,0:T(8,128)} %all-reduce.2.cloned.1.call-done), kind=kLoop, calls=%fused_computation.7 | loop fusion | flops 1572863 | bytes 3145732 | tf_op jit(solution)/shard_map/reduce_sum | solution.py:200
  246.5 2.7 %multiply_reduce_fusion.1 = f32[]{:T(128)} fusion(f32[3584,512]{1,0:T(8,128)} %all-reduce.2.cloned.1.call-done), kind=kLoop, calls=%fused_computation.19 | loop fusion | flops 1048575 | bytes 2097156 | tf_op jit(solution)/shard_map/reduce_sum | solution.py:200
  249.9 2.5 multiply_reduce_fusion.5
  253.8 2.3 slice_multiply_fusion
  256.1 1.9 slice_multiply_fusion.1
  258.0 1.8 slice_multiply_fusion.3
  259.8 0.7 maximum_bitcast_fusion
  260.5 1.9 copy.54
  262.4 0.7 dynamic_slice.5
  (94 shorter events, 6.1 us)
Async XLA Ops:
  8.0 29.1 %copy-start = (bf16[1536,512]{1,0:T(8,128)(2,1)S(1)}, bf16[1536,512]{1,0:T(8,128)(2,1)}, u32[]{:S(2)}) copy-start(bf16[1536,512]{1,0:T(8,128)(2,1)} %param.17) | copy-start | bytes 4718596
  8.0 60.5 %sort.19.cloned.1.call-start = ((), (), s32[]{:S(2)}) async-start(), calls=%async_computation.1 | async-start | bytes 24608 | tf_op jit(solution)/shard_map/jit(argsort)/sort | solution.py:165
  11.5 11.3 %copy-start.19 = (s32[1,1,6,128]{3,1,2,0:T(1,128)S(1)}, s32[1,1,6,128]{3,1,2,0:T(1,128)}, u32[]{:S(2)}) copy-start(s32[1,1,6,128]{3,1,2,0:T(1,128)} %param.29) | copy-start | bytes 9220
  11.5 12.6 %copy-start.21 = (s32[1,1,6]{2,1,0:T(1,128)S(1)}, s32[1,1,6]{2,1,0:T(1,128)}, u32[]{:S(2)}) copy-start(s32[1,1,6]{2,1,0:T(1,128)} %param.27) | copy-start | bytes 76
  11.6 12.7 %copy-start.22 = (s32[1,1,6]{2,1,0:T(1,128)S(1)}, s32[1,1,6]{2,1,0:T(1,128)}, u32[]{:S(2)}) copy-start(s32[1,1,6]{2,1,0:T(1,128)} %param.28) | copy-start | bytes 76
  11.6 12.8 %copy-start.11 = (bf16[1,1,256,512]{3,2,1,0:T(8,128)(2,1)S(1)}, bf16[1,1,256,512]{3,2,1,0:T(8,128)(2,1)}, u32[]{:S(2)}) copy-start(bf16[1,1,256,512]{3,2,1,0:T(8,128)(2,1)} %param.23) | copy-start | bytes 786436
  11.6 12.9 %copy-start.1 = (bf16[1,1,256,512]{3,2,1,0:T(8,128)(2,1)S(1)}, bf16[1,1,256,512]{3,2,1,0:T(8,128)(2,1)}, u32[]{:S(2)}) copy-start(bf16[1,1,256,512]{3,2,1,0:T(8,128)(2,1)} %param.15) | copy-start | bytes 786436
  12.6 16.4 %collective-permute-start = (bf16[1,2,128,512]{3,2,1,0:T(8,128)(2,1)}, bf16[1,2,128,512]{3,2,1,0:T(8,128)(2,1)}, u32[]{:S(2)}, u32[]{:S(2)}) collective-permute-start(bf16[1,2,128,512]{3,2,1,0:T(8,128)(2,1)} %get-tuple-element.28), channel_id=1, source_target_pairs={{0,2},{2,4},{4,6},{6,8},{8,10},{10,12},{12,14},{14,16},{16,18},{18... | collective-permute-start | bytes 786440 | tf_op jit(solution)/shard_map/ppermute | solution.py:12
  18.1 12.7 %collective-permute-start.1 = (bf16[1,2,128,512]{3,2,1,0:T(8,128)(2,1)}, bf16[1,2,128,512]{3,2,1,0:T(8,128)(2,1)}, u32[]{:S(2)}, u32[]{:S(2)}) collective-permute-start(bf16[1,2,128,512]{3,2,1,0:T(8,128)(2,1)} %get-tuple-element.27), channel_id=1, source_target_pairs={{2,0},{4,2},{6,4},{8,6},{10,8},{12,10},{14,12},{16,14},{18,16},{20... | collective-permute-start | bytes 786440 | tf_op jit(solution)/shard_map/ppermute | solution.py:15
  19.4 12.4 %collective-permute-start.2 = (bf16[1,2,128,512]{3,2,1,0:T(8,128)(2,1)}, bf16[1,2,128,512]{3,2,1,0:T(8,128)(2,1)}, u32[]{:S(2)}, u32[]{:S(2)}) collective-permute-start(bf16[1,2,128,512]{3,2,1,0:T(8,128)(2,1)} %get-tuple-element.26), channel_id=1, source_target_pairs={{0,1},{2,3},{4,5},{6,7},{8,9},{10,11},{12,13},{14,15},{16,17},{18,... | collective-permute-start | bytes 786440 | tf_op jit(solution)/shard_map/ppermute | solution.py:12
  21.6 11.2 %collective-permute-start.3 = (bf16[1,2,128,512]{3,2,1,0:T(8,128)(2,1)}, bf16[1,2,128,512]{3,2,1,0:T(8,128)(2,1)}, u32[]{:S(2)}, u32[]{:S(2)}) collective-permute-start(bf16[1,2,128,512]{3,2,1,0:T(8,128)(2,1)} %get-tuple-element.25), channel_id=1, source_target_pairs={{1,0},{3,2},{5,4},{7,6},{9,8},{11,10},{13,12},{15,14},{17,16},{19,... | collective-permute-start | bytes 786440 | tf_op jit(solution)/shard_map/ppermute | solution.py:15
  24.1 218.4 %all-reduce.2.cloned.1.call-start = ((), (), s32[]{:S(2)}) async-start(), calls=%async_computation | async-start | bytes 14680064 | tf_op jit(solution)/shard_map/psum | solution.py:195
  33.8 3.3 %copy-start.26 = (f32[512]{0:T(512)S(1)}, f32[512]{0:T(512)}, u32[]{:S(2)}) copy-start(f32[512]{0:T(512)} %param.18) | copy-start | bytes 6148
  37.1 4.3 %copy-start.17 = (bf16[512,512]{1,0:T(8,128)(2,1)S(1)}, bf16[512,512]{1,0:T(8,128)(2,1)}, u32[]{:S(2)}) copy-start(bf16[512,512]{1,0:T(8,128)(2,1)} %param.19) | copy-start | bytes 1572868
  41.5 1.0 copy-start.9
  42.1 1.1 copy-start.2
  43.3 2.0 copy-start.14
  43.3 2.0 copy-start.25
  45.2 1.0 copy-start.24
  53.0 3.2 %copy-start.7 = (bf16[1,1,768,512]{3,2,1,0:T(8,128)(2,1)S(1)}, bf16[1,1,768,512]{3,2,1,0:T(8,128)(2,1)}, u32[]{:S(2)}) copy-start(bf16[1,1,768,512]{3,2,1,0:T(8,128)(2,1)} %param.24) | copy-start | bytes 2359300
  56.1 2.7 %copy-start.3 = (f32[768,512]{1,0:T(8,128)S(1)}, f32[768,512]{1,0:T(8,128)}, u32[]{:S(2)}) copy-start(f32[768,512]{1,0:T(8,128)} %copy-done.2) | copy-start | bytes 4718596
  56.1 2.8 %copy-start.4 = (f32[768,512]{1,0:T(8,128)S(1)}, f32[768,512]{1,0:T(8,128)}, u32[]{:S(2)}) copy-start(f32[768,512]{1,0:T(8,128)} %gather_fusion.3) | copy-start | bytes 4718596
  58.9 1.1 copy-start.10
  60.1 1.0 copy-start.18
  60.1 1.6 copy-start.27
  61.7 1.1 copy-start.15
  61.7 1.4 copy-start.16
  61.7 1.6 copy-start.23
  63.3 1.6 copy-start.6
  63.3 1.9 copy-start.13
  70.1 1.4 copy-start.8
  86.0 9.6 %copy-start.5 = (f32[768,512]{1,0:T(8,128)S(1)}, f32[768,512]{1,0:T(8,128)}, u32[]{:S(2)}) copy-start(f32[768,512]{1,0:T(8,128)} %get-tuple-element.13) | copy-start | bytes 4718596
  86.8 17.3 %collective-permute-start.4 = (bf16[1,2,128,512]{3,1,2,0:T(2,128)(2,1)S(1)}, bf16[1,2,128,512]{3,1,2,0:T(2,128)(2,1)S(1)}, u32[]{:S(2)}, u32[]{:S(2)}) collective-permute-start(bf16[1,2,128,512]{3,1,2,0:T(2,128)(2,1)S(1)} %get-tuple-element.15), channel_id=1, source_target_pairs={{0,2},{2,4},{4,6},{6,8},{8,10},{10,12},{12,14},{14,16},{16,18},{18... | collective-permute-start | bytes 786440 | tf_op jit(solution)/shard_map/ppermute | solution.py:12
  90.3 17.5 %collective-permute-start.5 = (bf16[1,2,128,512]{3,1,2,0:T(2,128)(2,1)S(1)}, bf16[1,2,128,512]{3,1,2,0:T(2,128)(2,1)S(1)}, u32[]{:S(2)}, u32[]{:S(2)}) collective-permute-start(bf16[1,2,128,512]{3,1,2,0:T(2,128)(2,1)S(1)} %get-tuple-element.18), channel_id=1, source_target_pairs={{2,0},{4,2},{6,4},{8,6},{10,8},{12,10},{14,12},{16,14},{18,16},{20... | collective-permute-start | bytes 786440 | tf_op jit(solution)/shard_map/ppermute | solution.py:15
  91.6 16.8 %collective-permute-start.6 = (bf16[1,2,128,512]{3,1,2,0:T(2,128)(2,1)S(1)}, bf16[1,2,128,512]{3,1,2,0:T(2,128)(2,1)S(1)}, u32[]{:S(2)}, u32[]{:S(2)}) collective-permute-start(bf16[1,2,128,512]{3,1,2,0:T(2,128)(2,1)S(1)} %get-tuple-element.17), channel_id=1, source_target_pairs={{0,1},{2,3},{4,5},{6,7},{8,9},{10,11},{12,13},{14,15},{16,17},{18,... | collective-permute-start | bytes 786440 | tf_op jit(solution)/shard_map/ppermute | solution.py:12
  94.1 14.3 %collective-permute-start.7 = (bf16[1,2,128,512]{3,1,2,0:T(2,128)(2,1)S(1)}, bf16[1,2,128,512]{3,1,2,0:T(2,128)(2,1)S(1)}, u32[]{:S(2)}, u32[]{:S(2)}) collective-permute-start(bf16[1,2,128,512]{3,1,2,0:T(2,128)(2,1)S(1)} %get-tuple-element.16), channel_id=1, source_target_pairs={{1,0},{3,2},{5,4},{7,6},{9,8},{11,10},{13,12},{15,14},{17,16},{19,... | collective-permute-start | bytes 786440 | tf_op jit(solution)/shard_map/ppermute | solution.py:15
  109.0 1.2 copy-start.20
  110.1 3.3 %copy-start.12 = (f32[256,512]{1,0:T(8,128)S(1)}, f32[256,512]{1,0:T(8,128)}, u32[]{:S(2)}) copy-start(f32[256,512]{1,0:T(8,128)} %get-tuple-element.24) | copy-start | bytes 1572868
Sparse Core Ops, SparseCore 0:
  24.2 2.3 sort.21.cloned.1.call-done
  (1 shorter events, 0.0 us)
Sparse Core Ops, SparseCore 1:
  68.6 173.8 all-reduce.1
where the time goes:
time: 271 us
  waiting for transfers between devices  140 us (52%)
  local copies, waits for them, and re-layouts  34.2 us (13%)
  other arithmetic  32 us (12%)
  matrix products  26.2 us (10%)
  starting transfers between devices  19.1 us (7%)
  between operations  18.9 us (7%)
    psum x1, waiting for transfers between devices, on_device(): summed = lax.psum(weight_grad, ('gx', 'gy'))  128 us
    ppermute x4, starting transfers between devices, padded(): lax.ppermute(lax.slice_in_dim(block, block.shape[dim] - width, None, axis...  13.7 us
    unnamed x64, local copies, waits for them, and re-layouts  9.38 us
    reduce_sum x3, other arithmetic, on_device(): pieces.append(matrix * lax.rsqrt(jnp.mean(matrix * matrix) + 1e-06))  8.52 us
    gather x1, local copies, waits for them, and re-layouts, on_device(): jnp.take_along_axis(grad_s.reshape(tile_count, block_size, feature), inve...  7.83 us
    ppermute x4, waiting for transfers between devices, padded(): lax.ppermute(lax.slice_in_dim(block, block.shape[dim] - width, None, axis...  7.47 us
    mul x3, other arithmetic, on_device(): pieces.append(matrix * lax.rsqrt(jnp.mean(matrix * matrix) + 1e-06))  5.99 us
    dot_general x4, matrix products, matmul(): return jnp.dot(factor, second, preferred_element_type=jnp.float32)  5.82 us
  transfers between devices with their start and end apart: 9, of which 5 were waited for; matrix products, arithmetic and copies ran while one was open for 13% of the time, Pallas kernels for 0%

commit v1 on v0

--- a/solution.py
+++ b/solution.py
@@ -192,7 +192,7 @@
     weight_grad = jnp.concatenate([g_ew1, g_ew2, g_nw1, g_nw2], axis=0)
     total_entries = 7 * feature * feature
     share_len = total_entries // lax.axis_size(("gx", "gy"))
-    summed = lax.psum(weight_grad, ("gx", "gy"))
+    summed = lax.psum(lax.psum(weight_grad, "gy"), "gx")
     bounds = [0, 3 * feature, 4 * feature, 6 * feature, 7 * feature]
     pieces = []
     for index in range(4):

time: 271 us -> 377 us (1.39)
  waiting for transfers between devices: 140 us -> 246 us
    psum x1 -> x2, waiting for transfers between devices: 128 us -> 236 us  [on_device(): summed = lax.psum(lax.psum(weight_grad, 'gy'), 'gx')]
    ppermute x4, waiting for transfers between devices: 7.47 us -> 2.31 us  [padded(): lax.ppermute(lax.slice_in_dim(block, block.shape[dim] - width, None, axis...]
  transfers between devices with their start and end apart: 9 -> 10, of which waited for: 5 -> 5; matrix products, arithmetic and copies ran while one was open for 13% -> 9% of each run, Pallas kernels for 0% -> 0%
where the time goes in v1:
time: 377 us; the launch traced here: 376 us
  waiting for transfers between devices  246 us (65%)
  local copies, waits for them, and re-layouts  34.2 us (9%)
  other arithmetic  32 us (8%)
  matrix products  26.4 us (7%)
  starting transfers between devices  18.8 us (5%)
  between operations  18.8 us (5%)
    psum x2, waiting for transfers between devices, on_device(): summed = lax.psum(lax.psum(weight_grad, 'gy'), 'gx')  236 us
    ppermute x4, starting transfers between devices, padded(): lax.ppermute(lax.slice_in_dim(block, block.shape[dim] - width, None, axis...  13.3 us
    unnamed x64, local copies, waits for them, and re-layouts  9.38 us
    reduce_sum x3, other arithmetic, on_device(): pieces.append(matrix * lax.rsqrt(jnp.mean(matrix * matrix) + 1e-06))  8.51 us
    gather x1, local copies, waits for them, and re-layouts, on_device(): jnp.take_along_axis(grad_s.reshape(tile_count, block_size, feature), inve...  7.83 us
    ppermute x4, waiting for transfers between devices, padded(): lax.ppermute(lax.slice_in_dim(block, 0, width, axis=dim), axis, backward)  7.73 us
  transfers between devices with their start and end apart: 10, of which 5 were waited for; matrix products, arithmetic and copies ran while one was open for 9% of the time, Pallas kernels for 0%

profile of v1, /device:TPU:0, one launch (start us, length us, event | category | flops | bytes accessed | tf_op | source)
XLA Modules:
  0.0 376.5 jit_solution(8669624442300811124)
XLA Ops:
  8.1 0.8 compare_select_fusion.3
  9.0 0.7 iota_compare_fusion.1
  9.8 1.6 gather_fusion.1
  11.6 1.0 fusion.59
  12.6 5.6 %collective-permute-start = (bf16[1,2,128,512]{3,2,1,0:T(8,128)(2,1)}, bf16[1,2,128,512]{3,2,1,0:T(8,128)(2,1)}, u32[]{:S(2)}, u32[]{:S(2)}) collective-permute-start(bf16[1,2,128,512]{3,2,1,0:T(8,128)(2,1)} %get-tuple-element.28), channel_id=1, source_target_pairs={{0,2},{2,4},{4,6},{6,8},{8,10},{10,12},{12,14},{14,16},{16,18},{18... | collective-permute-start | bytes 786440 | tf_op jit(solution)/shard_map/ppermute | solution.py:12
  18.1 1.3 collective-permute-start.1
  19.4 2.2 collective-permute-start.2
  21.6 1.3 collective-permute-start.3
  23.3 3.4 gather_fusion
  26.6 2.3 collective-permute-done
  28.9 1.0 bitcast_dynamic-update-slice_fusion.3
  29.9 0.9 collective-permute-done.1
  30.9 1.0 bitcast_dynamic-update-slice_fusion.2
  31.8 1.0 bitcast_dynamic-update-slice_fusion.1
  32.8 1.0 bitcast_dynamic-update-slice_fusion
  33.8 3.3 gather_fusion.2
  37.1 4.3 %multiply_convert_fusion.2 = (bf16[768,512]{1,0:T(8,128)(2,1)S(1)}, f32[768,512]{1,0:T(8,128)}) fusion(f32[512]{0:T(512)S(1)} %copy-done.26, bf16[1536,512]{1,0:T(8,128)(2,1)S(1)} %copy-done, bf16[768,512]{1,0:T(8,128)(2,1)} %gather_fusion.2, bf16[768,512]{1,0:T(8,128)(2,1)} %gather_fusion, bf16[768,512]{1,0:T(8,128)(2,1)} %bitcast.150), kind=kOutput, calls=%fused_computation.28 | convolution fusion | flops 1217396736 | bytes 6293504 | tf_op jit(solution)/shard_map/dot_general | solution.py:52
  41.5 0.6 fusion.60
  43.3 1.9 fusion.12
  45.7 0.5 copy-done.24
  46.9 0.9 fusion.28
  47.8 1.5 fusion.54
  50.3 1.8 fusion.29
  52.1 0.9 fusion.58
  53.0 3.2 gather_fusion.3
  56.1 2.7 fusion.20
  58.9 0.5 multiply_convert_fusion.1
  59.5 0.6 copy-done.10
  60.1 0.6 fusion.65
  61.1 0.5 copy-done.27
  61.7 0.9 multiply_convert_fusion
  63.3 1.4 fusion.17
  65.1 3.4 pad_maximum_fusion
  68.6 0.6 copy.83
  69.2 0.6 iota.34
  69.8 33.5 %all-reduce.3.cloned.1.call-done = f32[3584,512]{1,0:T(8,128)} async-done(((f32[3584,512]{1,0:T(8,128)}), f32[3584,512]{1,0:T(8,128)}) %all-reduce.3.cloned.1.call-update) | async-done | bytes 7340048 | tf_op jit(solution)/shard_map/psum | solution.py:195
  103.4 0.7 compare_and_fusion
  104.2 0.7 fusion.33
  104.9 1.4 fusion.64
  106.3 1.9 fusion.19
  108.2 7.8 %gather_fusion.4 = f32[768,512]{1,0:T(8,128)} fusion(f32[6,128,512]{2,1,0:T(8,128)S(1)} %bitcast.133, s32[768]{0:T(1024)S(1)} %fusion.33), kind=kCustom, calls=%fused_computation.4 | custom fusion | bytes 3151872 | tf_op jit(solution)/shard_map/jit(take_along_axis)/gather | solution.py:166
  116.1 4.9 %fusion.62 = (bf16[10,128,512]{2,0,1:T(8,128)(2,1)S(1)}, f32[10,128,512]{2,0,1:T(8,128)S(1)}) fusion(f32[6,128,512]{2,1,0:T(8,128)} %bitcast.137, pred[6,128]{0,1:T(8,128)(4,1)S(1)} %copy.42, s32[6]{0:T(128)S(1)} %bitcast.149), kind=kOutput, calls=%fused_computation.139 | convolution fusion | flops 48234556 | bytes 5505816 | tf_op jit(solution)/shard_map/bt,tnf->bnf/dot_general | solution.py:173
  121.0 0.8 slice_bitcast_fusion.3
  121.8 3.7 collective-permute-start.4
  125.5 1.3 collective-permute-start.5
  126.8 1.9 collective-permute-start.6
  128.7 1.5 collective-permute-start.7
  130.2 1.9 fusion.2
  132.3 6.8 %collective-permute-done.5 = bf16[1,2,128,512]{3,1,2,0:T(2,128)(2,1)S(1)} collective-permute-done((bf16[1,2,128,512]{3,1,2,0:T(2,128)(2,1)S(1)}, bf16[1,2,128,512]{3,1,2,0:T(2,128)(2,1)S(1)}, u32[]{:S(2)}, u32[]{:S(2)}) %collective-permute-start.5) | collective-permute-done | bytes 262176 | tf_op jit(solution)/shard_map/ppermute | solution.py:15
  139.1 0.6 maximum_convert_fusion.1
  139.7 0.6 maximum_convert_fusion
  140.4 1.1 pad_maximum_fusion.2
  141.5 3.2 fusion.8
  144.8 1.0 fusion.24
  145.8 202.8 %all-reduce.5.cloned.1.call-done = f32[3584,512]{1,0:T(8,128)} async-done(((f32[3584,512]{1,0:T(8,128)}), f32[3584,512]{1,0:T(8,128)}) %all-reduce.5.cloned.1.call-update) | async-done | bytes 7340048 | tf_op jit(solution)/shard_map/psum | solution.py:195
  348.6 3.3 multiply_reduce_fusion
  352.6 2.7 multiply_reduce_fusion.1
  356.0 2.5 multiply_reduce_fusion.5
  359.8 2.3 slice_multiply_fusion
  362.1 1.9 slice_multiply_fusion.1
  364.0 1.8 slice_multiply_fusion.3
  365.8 0.7 maximum_bitcast_fusion
  366.5 1.9 copy.54
  368.4 0.7 dynamic_slice.5
  (97 shorter events, 6.2 us)
Async XLA Ops:
  8.0 29.1 %copy-start = (bf16[1536,512]{1,0:T(8,128)(2,1)S(1)}, bf16[1536,512]{1,0:T(8,128)(2,1)}, u32[]{:S(2)}) copy-start(bf16[1536,512]{1,0:T(8,128)(2,1)} %param.17) | copy-start | bytes 4718596
  8.0 95.3 %all-reduce.3.cloned.1.call-start = ((), (), s32[]{:S(2)}) async-start(), calls=%async_computation | async-start | bytes 14680064 | tf_op jit(solution)/shard_map/psum | solution.py:195
  11.5 11.3 %copy-start.21 = (s32[1,1,6]{2,1,0:T(1,128)S(1)}, s32[1,1,6]{2,1,0:T(1,128)}, u32[]{:S(2)}) copy-start(s32[1,1,6]{2,1,0:T(1,128)} %param.27) | copy-start | bytes 76
  11.5 11.4 %copy-start.22 = (s32[1,1,6]{2,1,0:T(1,128)S(1)}, s32[1,1,6]{2,1,0:T(1,128)}, u32[]{:S(2)}) copy-start(s32[1,1,6]{2,1,0:T(1,128)} %param.28) | copy-start | bytes 76
  11.6 11.5 %copy-start.11 = (bf16[1,1,256,512]{3,2,1,0:T(8,128)(2,1)S(1)}, bf16[1,1,256,512]{3,2,1,0:T(8,128)(2,1)}, u32[]{:S(2)}) copy-start(bf16[1,1,256,512]{3,2,1,0:T(8,128)(2,1)} %param.23) | copy-start | bytes 786436
  11.6 11.6 %copy-start.19 = (s32[1,1,6,128]{3,1,2,0:T(1,128)S(1)}, s32[1,1,6,128]{3,1,2,0:T(1,128)}, u32[]{:S(2)}) copy-start(s32[1,1,6,128]{3,1,2,0:T(1,128)} %param.29) | copy-start | bytes 9220
  11.6 11.7 %copy-start.1 = (bf16[1,1,256,512]{3,2,1,0:T(8,128)(2,1)S(1)}, bf16[1,1,256,512]{3,2,1,0:T(8,128)(2,1)}, u32[]{:S(2)}) copy-start(bf16[1,1,256,512]{3,2,1,0:T(8,128)(2,1)} %param.15) | copy-start | bytes 786436
  12.6 16.4 %collective-permute-start = (bf16[1,2,128,512]{3,2,1,0:T(8,128)(2,1)}, bf16[1,2,128,512]{3,2,1,0:T(8,128)(2,1)}, u32[]{:S(2)}, u32[]{:S(2)}) collective-permute-start(bf16[1,2,128,512]{3,2,1,0:T(8,128)(2,1)} %get-tuple-element.28), channel_id=1, source_target_pairs={{0,2},{2,4},{4,6},{6,8},{8,10},{10,12},{12,14},{14,16},{16,18},{18... | collective-permute-start | bytes 786440 | tf_op jit(solution)/shard_map/ppermute | solution.py:12
  18.1 12.7 %collective-permute-start.1 = (bf16[1,2,128,512]{3,2,1,0:T(8,128)(2,1)}, bf16[1,2,128,512]{3,2,1,0:T(8,128)(2,1)}, u32[]{:S(2)}, u32[]{:S(2)}) collective-permute-start(bf16[1,2,128,512]{3,2,1,0:T(8,128)(2,1)} %get-tuple-element.27), channel_id=1, source_target_pairs={{2,0},{4,2},{6,4},{8,6},{10,8},{12,10},{14,12},{16,14},{18,16},{20... | collective-permute-start | bytes 786440 | tf_op jit(solution)/shard_map/ppermute | solution.py:15
  19.4 12.4 %collective-permute-start.2 = (bf16[1,2,128,512]{3,2,1,0:T(8,128)(2,1)}, bf16[1,2,128,512]{3,2,1,0:T(8,128)(2,1)}, u32[]{:S(2)}, u32[]{:S(2)}) collective-permute-start(bf16[1,2,128,512]{3,2,1,0:T(8,128)(2,1)} %get-tuple-element.26), channel_id=1, source_target_pairs={{0,1},{2,3},{4,5},{6,7},{8,9},{10,11},{12,13},{14,15},{16,17},{18,... | collective-permute-start | bytes 786440 | tf_op jit(solution)/shard_map/ppermute | solution.py:12
  21.6 11.2 %collective-permute-start.3 = (bf16[1,2,128,512]{3,2,1,0:T(8,128)(2,1)}, bf16[1,2,128,512]{3,2,1,0:T(8,128)(2,1)}, u32[]{:S(2)}, u32[]{:S(2)}) collective-permute-start(bf16[1,2,128,512]{3,2,1,0:T(8,128)(2,1)} %get-tuple-element.25), channel_id=1, source_target_pairs={{1,0},{3,2},{5,4},{7,6},{9,8},{11,10},{13,12},{15,14},{17,16},{19,... | collective-permute-start | bytes 786440 | tf_op jit(solution)/shard_map/ppermute | solution.py:15
  33.8 3.3 copy-start.26
  37.1 4.3 %copy-start.17 = (bf16[512,512]{1,0:T(8,128)(2,1)S(1)}, bf16[512,512]{1,0:T(8,128)(2,1)}, u32[]{:S(2)}) copy-start(bf16[512,512]{1,0:T(8,128)(2,1)} %param.19) | copy-start | bytes 1572868
  41.5 1.0 copy-start.9
  42.1 1.1 copy-start.2
  43.3 2.0 copy-start.14
  43.3 2.0 copy-start.25
  45.2 1.0 copy-start.24
  53.0 3.2 copy-start.7
  56.1 2.7 copy-start.3
  56.1 2.8 copy-start.4
  58.9 1.1 copy-start.10
  60.1 1.0 copy-start.18
  60.1 1.6 copy-start.27
  61.7 1.1 copy-start.15
  61.7 1.4 copy-start.16
  61.7 1.6 copy-start.23
  63.3 1.6 copy-start.6
  63.3 1.9 copy-start.13
  68.5 34.9 %sort.19.cloned.1.call-start = ((), (), s32[]{:S(2)}) async-start(), calls=%async_computation.2 | async-start | bytes 24608 | tf_op jit(solution)/shard_map/jit(argsort)/sort | solution.py:165
  69.8 278.8 %all-reduce.5.cloned.1.call-start = ((), (), s32[]{:S(2)}) async-start(), calls=%async_computation.1 | async-start | bytes 14680064 | tf_op jit(solution)/shard_map/psum | solution.py:195
  104.9 1.4 copy-start.8
  121.0 9.2 %copy-start.5 = (f32[768,512]{1,0:T(8,128)S(1)}, f32[768,512]{1,0:T(8,128)}, u32[]{:S(2)}) copy-start(f32[768,512]{1,0:T(8,128)} %get-tuple-element.13) | copy-start | bytes 4718596
  121.8 10.5 %collective-permute-start.4 = (bf16[1,2,128,512]{3,1,2,0:T(2,128)(2,1)S(1)}, bf16[1,2,128,512]{3,1,2,0:T(2,128)(2,1)S(1)}, u32[]{:S(2)}, u32[]{:S(2)}) collective-permute-start(bf16[1,2,128,512]{3,1,2,0:T(2,128)(2,1)S(1)} %get-tuple-element.15), channel_id=1, source_target_pairs={{0,2},{2,4},{4,6},{6,8},{8,10},{10,12},{12,14},{14,16},{16,18},{18... | collective-permute-start | bytes 786440 | tf_op jit(solution)/shard_map/ppermute | solution.py:12
  125.5 13.6 %collective-permute-start.5 = (bf16[1,2,128,512]{3,1,2,0:T(2,128)(2,1)S(1)}, bf16[1,2,128,512]{3,1,2,0:T(2,128)(2,1)S(1)}, u32[]{:S(2)}, u32[]{:S(2)}) collective-permute-start(bf16[1,2,128,512]{3,1,2,0:T(2,128)(2,1)S(1)} %get-tuple-element.18), channel_id=1, source_target_pairs={{2,0},{4,2},{6,4},{8,6},{10,8},{12,10},{14,12},{16,14},{18,16},{20... | collective-permute-start | bytes 786440 | tf_op jit(solution)/shard_map/ppermute | solution.py:15
  126.8 12.9 %collective-permute-start.6 = (bf16[1,2,128,512]{3,1,2,0:T(2,128)(2,1)S(1)}, bf16[1,2,128,512]{3,1,2,0:T(2,128)(2,1)S(1)}, u32[]{:S(2)}, u32[]{:S(2)}) collective-permute-start(bf16[1,2,128,512]{3,1,2,0:T(2,128)(2,1)S(1)} %get-tuple-element.17), channel_id=1, source_target_pairs={{0,1},{2,3},{4,5},{6,7},{8,9},{10,11},{12,13},{14,15},{16,17},{18,... | collective-permute-start | bytes 786440 | tf_op jit(solution)/shard_map/ppermute | solution.py:12
  128.7 11.0 %collective-permute-start.7 = (bf16[1,2,128,512]{3,1,2,0:T(2,128)(2,1)S(1)}, bf16[1,2,128,512]{3,1,2,0:T(2,128)(2,1)S(1)}, u32[]{:S(2)}, u32[]{:S(2)}) collective-permute-start(bf16[1,2,128,512]{3,1,2,0:T(2,128)(2,1)S(1)} %get-tuple-element.16), channel_id=1, source_target_pairs={{1,0},{3,2},{5,4},{7,6},{9,8},{11,10},{13,12},{15,14},{17,16},{19,... | collective-permute-start | bytes 786440 | tf_op jit(solution)/shard_map/ppermute | solution.py:15
  140.4 1.2 copy-start.20
  141.5 3.3 copy-start.12
Sparse Core Ops, SparseCore 0:
  68.7 34.6 all-reduce.2
  109.4 239.1 all-reduce.4
Sparse Core Ops, SparseCore 1:
  71.8 2.2 sort.21.cloned.1.call-done
  (1 shorter events, 0.0 us)
